TPU v7x, 256 devices: a whole 4x4x8 slice. The times are simulated.
256 devices in a mesh: section: 8 (over z), dp: 32 (over x, y, core).
Axes of the slice: x: 4, y: 4, z: 8, core: 2. Of those that a mesh axis runs over, the one named last changes fastest.
Arguments:
- output_gradient: bfloat16 [8, 4096, 2048], P('section', 'dp'), may hold values from -6 to 6
- saved_input: bfloat16 [8, 4096, 8192], P('section', 'dp'), may hold values from -6 to 6
- frozen_matrix: bfloat16 [8, 8192, 2048], P('section', 'dp'), may hold values from -0.0625 to 0.0625
- adapter_down_maps: bfloat16 [8, 8192, 2048], P('section', None, 'dp'), may hold values from -0.0625 to 0.0625
- adapter_up_maps: bfloat16 [8, 2048, 2048], P('section', None, 'dp'), may hold values from -0.125 to 0.125
- token_tenants: int32 [8, 4096], P('section'), may hold values from 0 to 31, never falling along the last dimension, each value on 1 to 256 neighbouring positions
- tenant_slot_lookup: int32 [8, 32], P('section'), may hold values from 0 to 31, each once within a row
Outputs:
- passed_grad: bfloat16 [8, 4096, 8192], P('section', 'dp')
- down_gradient: bfloat16 [8, 8192, 2048], P('section', None, 'dp')
- up_gradient: bfloat16 [8, 2048, 2048], P('section', None, 'dp')
Inputs may be any that keep to these rules, and one draw needn't show every extreme that they name: `token_tenants`: within a section the ids never fall; each of the 32 tenants has 1 to 256 tokens, one exactly 256. `tenant_slot_lookup`: each section's row is a permutation.
All inputs are finite; a program needn't handle non-finite values.
Results may differ from a plain program's by a relative error of at most 0.005.
Values may be sent and summed in bfloat16 or wider, within the bound.
A program may use at most 128 MiB of HBM per device.

v0:
```python
import jax
import jax.numpy as jnp
from jax import lax
from jax.sharding import PartitionSpec as P

ADAPTER_RANK = 64
MOST = 256
adapter_scale = 2.0


def from_behind(value, axis, steps):
    count = lax.axis_size(axis)
    first, last = (max(0, -steps), min(count, count - steps))
    return lax.ppermute(value, axis, [(source, source + steps) for source in range(first, last)])


def block_layout(tenant_row, slot_table, tenants, most):
    tokens = tenant_row.shape[0]
    tenant_range = jnp.arange(tenants, dtype=jnp.int32)
    member = (tenant_range[:, None] == tenant_row[None, :]).astype(jnp.int32)
    counts = jnp.sum(member, axis=1)
    starts = jnp.cumsum(counts) - counts
    owner_match = (slot_table[None, :] == tenant_range[:, None]).astype(jnp.int32)
    slot_start = jnp.sum(owner_match * starts[None, :], axis=1)
    slot_count = jnp.sum(owner_match * counts[None, :], axis=1)
    place = jnp.arange(most, dtype=jnp.int32)
    live_slot = place[None, :] < slot_count[:, None]
    row_index = jnp.minimum(slot_start[:, None] + place[None, :], tokens - 1)
    token_slot = jnp.sum(member * slot_table[:, None], axis=0)
    token_start = jnp.sum(member * starts[:, None], axis=0)
    token_place = token_slot * most + jnp.arange(tokens, dtype=jnp.int32) - token_start
    return (row_index, live_slot, token_place)


def masked_rows(rows, row_index, live_slot):
    picked = rows[row_index]
    return jnp.where(live_slot[:, :, None], picked, jnp.zeros((), picked.dtype))


def adapter_term(rank_up_values, down_three, token_place):
    blocks = jnp.einsum(
        "kpr,dkr->kpd", rank_up_values, down_three, preferred_element_type=jnp.float32
    )
    return blocks.reshape(blocks.shape[0] * blocks.shape[1], blocks.shape[2])[token_place]


def local(
    output_gradient,
    saved_input,
    frozen_matrix,
    adapter_down_maps,
    adapter_up_maps,
    token_tenants,
    tenant_slot_lookup,
):
    grad_rows = output_gradient[0]
    saved_rows = saved_input[0]
    weight = frozen_matrix[0]
    local_width = weight.shape[0]
    out_width = weight.shape[1]
    kv_local = out_width // lax.axis_size("dp")
    kv_offset = lax.axis_index("dp") * kv_local
    tenants = tenant_slot_lookup.shape[1]
    contract_last = (((1,), (1,)), ((), ()))
    row_index, live_slot, token_place = block_layout(
        token_tenants[0], tenant_slot_lookup[0], tenants, MOST
    )
    saved_cols = lax.all_to_all(saved_rows, "dp", split_axis=1, concat_axis=0, tiled=True)
    saved_input_blocks = masked_rows(saved_cols, row_index, live_slot)
    block_rows = lax.all_gather(grad_rows, "dp", axis=0, tiled=True)
    frozen_part = lax.dot_general(
        block_rows, weight, contract_last, preferred_element_type=jnp.float32
    )
    own_cols = lax.dynamic_slice_in_dim(block_rows, kv_offset, kv_local, 1).astype(jnp.float32)
    joined = jnp.concatenate([frozen_part, own_cols], axis=1)
    frozen_product = joined[:, :local_width]
    grad_cols = joined[:, local_width:].astype(jnp.bfloat16)
    down_cols, up_cols = (
        lax.all_to_all(adapter_down_maps[0], "dp", split_axis=0, concat_axis=1, tiled=True),
        lax.all_to_all(adapter_up_maps[0], "dp", split_axis=0, concat_axis=1, tiled=True),
    )
    down_three = down_cols.reshape(local_width, tenants, ADAPTER_RANK)
    up_three = up_cols.reshape(kv_local, tenants, ADAPTER_RANK)
    gradient_blocks = masked_rows(grad_cols, row_index, live_slot)
    up_part = jnp.einsum(
        "kpe,ekr->kpr", gradient_blocks, up_three, preferred_element_type=jnp.float32
    )
    down_part = jnp.einsum(
        "kpd,dkr->kpr", saved_input_blocks, down_three, preferred_element_type=jnp.float32
    )
    up_total, down_total = lax.psum((up_part, down_part), "dp")
    rank_up_values = up_total.astype(jnp.bfloat16)
    rank_down_values = down_total.astype(jnp.bfloat16)
    adapter_slot = adapter_term(rank_up_values, down_three, token_place)
    down_grad_cols = (
        (
            adapter_scale
            * jnp.einsum(
                "tfv,tfy->vty",
                saved_input_blocks,
                rank_up_values,
                preferred_element_type=jnp.float32,
            )
        )
        .reshape(local_width, tenants * ADAPTER_RANK)
        .astype(jnp.bfloat16)
    )
    up_grad_cols = (
        (
            adapter_scale
            * jnp.einsum(
                "ohz,ohq->zoq",
                gradient_blocks,
                rank_down_values,
                preferred_element_type=jnp.float32,
            )
        )
        .reshape(kv_local, tenants * ADAPTER_RANK)
        .astype(jnp.bfloat16)
    )
    down_gradient, up_gradient = (
        lax.all_to_all(down_grad_cols, "dp", split_axis=1, concat_axis=0, tiled=True),
        lax.all_to_all(up_grad_cols, "dp", split_axis=1, concat_axis=0, tiled=True),
    )
    input_columns = (frozen_product + adapter_scale * adapter_slot).astype(jnp.bfloat16)
    input_rows = lax.all_to_all(input_columns, "dp", split_axis=0, concat_axis=1, tiled=True)
    passed = from_behind(input_rows, "section", -1)
    return (passed[None], down_gradient[None], up_gradient[None])


def solution(mesh):
    return jax.shard_map(
        local,
        mesh=mesh,
        in_specs=(
            P("section", "dp", None),
            P("section", "dp", None),
            P("section", "dp", None),
            P("section", None, "dp"),
            P("section", None, "dp"),
            P("section", None),
            P("section", None),
        ),
        out_specs=(P("section", "dp", None), P("section", None, "dp"), P("section", None, "dp")),
        check_vma=False,
    )
```

profile of v0, /device:TPU:1, one launch (start us, length us, event | category | flops | bytes accessed | tf_op | source)
XLA Modules:
  0.0 439.3 jit_solution(11001682472240546703)
XLA Ops:
  7.9 2.3 all_to_all.72
  10.2 2.0 copy.35
  12.2 2.1 reshape.196
  14.4 8.6 %all-to-all-start = ((bf16[32,2,2048]{2,1,0:T(2,128)(2,1)}), bf16[32,2,2048]{2,1,0:T(2,128)(2,1)S(1)}, u32[]{:S(2)}, u32[]{:S(2)}) async-start(bf16[32,2,2048]{2,1,0:T(2,128)(2,1)} %reshape.196), calls=%async_computation | async-start | bytes 524288 | tf_op jit(solution)/shard_map/all_to_all | solution.py:80
  23.6 2.5 copy.27
  26.1 6.0 %all-to-all-done = bf16[32,2,2048]{2,1,0:T(2,128)(2,1)S(1)} async-done(((bf16[32,2,2048]{2,1,0:T(2,128)(2,1)}), bf16[32,2,2048]{2,1,0:T(2,128)(2,1)S(1)}, u32[]{:S(2)}, u32[]{:S(2)}) %all-to-all-start) | async-done | bytes 262176 | tf_op jit(solution)/shard_map/all_to_all | solution.py:80
  32.1 3.8 all-to-all-start.3
  36.6 1.5 copy.32
  38.1 1.6 copy.25
  39.9 25.3 %all-to-all-done.3 = bf16[128,32,256]{2,0,1:T(8,128)(2,1)S(1)} async-done(((bf16[128,32,256]{2,0,1:T(8,128)(2,1)}), bf16[128,32,256]{2,0,1:T(8,128)(2,1)S(1)}, u32[]{:S(2)}, u32[]{:S(2)}) %all-to-all-start.3) | async-done | bytes 2097184 | tf_op jit(solution)/shard_map/all_to_all | solution.py:68
  65.2 5.5 %all-to-all-start.1 = ((bf16[32,256,64]{1,2,0:T(8,128)(2,1)}), bf16[32,256,64]{1,2,0:T(8,128)(2,1)}, u32[]{:S(2)}, u32[]{:S(2)}) async-start(bf16[32,256,64]{1,2,0:T(8,128)(2,1)} %copy.25), calls=%async_computation.1 | async-start | bytes 2097152 | tf_op jit(solution)/shard_map/all_to_all | solution.py:79
  72.0 33.1 %gather_fusion.2 = bf16[8192,256]{1,0:T(8,128)(2,1)} fusion(bf16[4096,256]{1,0:T(8,128)(2,1)S(1)} %bitcast.79, s32[8192]{0:T(1024)S(1)} %broadcast_clamp_fusion), kind=kCustom, calls=%fused_computation.2 | custom fusion | bytes 8421376 | tf_op jit(solution)/shard_map/gather | solution.py:36
  105.1 4.6 %fusion.8 = f32[32,256,64]{1,2,0:T(8,128)} fusion(bf16[32,256,256]{2,1,0:T(8,128)(2,1)} %bitcast.86, pred[32,256]{1,0:T(8,128)(4,1)S(1)} %iota_compare_fusion.1, bf16[32,256,64]{1,2,0:T(8,128)(2,1)} %all-to-all-done.1), kind=kOutput, calls=%fused_computation.8 | convolution fusion | flops 270532608 | bytes 7348224 | tf_op jit(solution)/shard_map/kpd,dkr->kpr/dot_general | solution.py:88
  109.7 12.3 %all-gather.3.cloned.1.call-done = bf16[1,4096,2048]{2,1,0:T(8,128)(2,1)} async-done(((bf16[1,128,2048]{2,1,0:T(8,128)(2,1)}), bf16[1,4096,2048]{2,1,0:T(8,128)(2,1)}) %all-gather.3.cloned.1.call-update) | async-done | bytes 16777232 | tf_op jit(solution)/shard_map/all_gather | solution.py:70
  122.0 1.6 dynamic-slice_bitcast_fusion
  123.5 29.5 %gather_fusion = bf16[8192,64]{1,0:T(8,128)(2,1)} fusion(bf16[4096,64]{1,0:T(8,128)(2,1)S(1)} %dynamic-slice_bitcast_fusion, s32[8192]{0:T(1024)S(1)} %broadcast_clamp_fusion), kind=kCustom, calls=%fused_computation | custom fusion | bytes 2129920 | tf_op jit(solution)/shard_map/gather | solution.py:36
  153.0 2.7 copy.23
  155.7 1.8 fusion.20
  157.5 146.1 %all-reduce.2 = (bf16[32,256,64]{1,2,0:T(8,128)(2,1)}, bf16[32,256,64]{1,2,0:T(8,128)(2,1)}) all-reduce(f32[32,256,64]{1,2,0:T(8,128)S(1)} %fusion.20, f32[32,256,64]{1,2,0:T(8,128)} %fusion.8), channel_id=1, replica_groups=mesh['section'=8,'dp'=32] {'dp'}, use_global_device_ids=true, to_apply=%region_4.5 | all-reduce | flops 1048576 | bytes 6291456 | tf_op jit(solution)/shard_map/psum | solution.py:91
  303.6 6.1 %fusion.16 = f32[32,256,256]{2,1,0:T(8,128)} fusion(bf16[32,256,64]{1,2,0:T(8,128)(2,1)} %all-to-all-done.1, bf16[32,256,64]{1,2,0:T(8,128)(2,1)} %get-tuple-element.7), kind=kOutput, calls=%fused_computation.18 | convolution fusion | flops 268435456 | bytes 10485760 | tf_op jit(solution)/shard_map/kpr,dkr->kpd/dot_general | solution.py:41
  309.7 19.5 %gather_fusion.1 = f32[4096,256]{1,0:T(8,128)} fusion(f32[8192,256]{1,0:T(8,128)} %bitcast.80, s32[4096]{0:T(1024)S(1)} %broadcast_clamp_fusion.1), kind=kCustom, calls=%fused_computation.1 | custom fusion | bytes 8404992 | tf_op jit(solution)/shard_map/gather | solution.py:44
  329.2 11.8 %fusion.5 = bf16[4096,256]{1,0:T(8,128)(2,1)S(1)} fusion(bf16[1,4096,2048]{2,1,0:T(8,128)(2,1)} %all-gather.3.cloned.1.call-done, f32[4096,256]{1,0:T(8,128)} %gather_fusion.1, bf16[1,256,2048]{2,1,0:T(8,128)(2,1)S(1)} %copy-done), kind=kOutput, calls=%fused_computation.6 | convolution fusion | flops 4298113024 | bytes 24117248 | tf_op jit(solution)/shard_map/dot_general | solution.py:71
  341.1 37.0 %all_to_all.96 = bf16[32,128,256]{2,1,0:T(8,128)(2,1)S(1)} all-to-all(bf16[32,128,256]{2,1,0:T(8,128)(2,1)S(1)} %bitcast.89), channel_id=1, replica_groups=mesh['section'=8,'dp'=32] {'dp'}, dimensions={0} | all-to-all | bytes 4194304 | tf_op jit(solution)/shard_map/all_to_all | solution.py:126
  378.1 1.5 copy.30
  382.5 3.9 all-to-all-start.5
  386.4 4.8 %fusion.12 = bf16[256,32,64]{0,2,1:T(8,128)(2,1)} fusion(bf16[32,256,256]{2,1,0:T(8,128)(2,1)} %bitcast.87, pred[32,256]{1,0:T(8,128)(4,1)S(1)} %iota_compare_fusion.1, bf16[32,256,64]{1,2,0:T(8,128)(2,1)S(1)} %copy-done.3), kind=kOutput, calls=%fused_computation.13 | convolution fusion | flops 271581184 | bytes 6299648 | tf_op jit(solution)/shard_map/tfv,tfy->vty/dot_general | solution.py:98
  391.2 4.2 all-to-all-done.5
  395.4 3.8 all-to-all-start.4
  401.1 15.1 %all-to-all-done.4 = bf16[256,32,64]{0,2,1:T(8,128)(2,1)S(1)} async-done(((bf16[256,32,64]{0,2,1:T(8,128)(2,1)}), bf16[256,32,64]{0,2,1:T(8,128)(2,1)S(1)}, u32[]{:S(2)}, u32[]{:S(2)}) %all-to-all-start.4) | async-done | bytes 1048608 | tf_op jit(solution)/shard_map/all_to_all | solution.py:122
  416.8 1.3 broadcast_in_dim.52
  418.1 11.3 %collective-permute-done = bf16[128,8192]{1,0:T(8,128)(2,1)} collective-permute-done((bf16[128,8192]{1,0:T(8,128)(2,1)}, bf16[128,8192]{1,0:T(8,128)(2,1)}, u32[]{:S(2)}, u32[]{:S(2)}) %collective-permute-start) | collective-permute-done | bytes 2097184 | tf_op jit(solution)/shard_map/ppermute | solution.py:14
  429.4 3.1 copy.41
  (41 shorter events, 8.8 us)
Async XLA Ops:
  7.2 322.1 %copy-start = (bf16[1,256,2048]{2,1,0:T(8,128)(2,1)S(1)}, bf16[1,256,2048]{2,1,0:T(8,128)(2,1)}, u32[]{:S(2)}) copy-start(bf16[1,256,2048]{2,1,0:T(8,128)(2,1)} %param.9) | copy-start | bytes 3145732
  7.2 15.8 %copy-start.2 = (bf16[1,128,8192]{2,1,0:T(8,128)(2,1)S(1)}, bf16[1,128,8192]{2,1,0:T(8,128)(2,1)}, u32[]{:S(2)}) copy-start(bf16[1,128,8192]{2,1,0:T(8,128)(2,1)} %param.8) | copy-start | bytes 6291460
  7.2 114.8 %all-gather.3.cloned.1.call-start = ((), (), s32[]{:S(2)}) async-start(), calls=%async_computation.6 | async-start | bytes 17301504 | tf_op jit(solution)/shard_map/all_gather | solution.py:70
  14.4 17.7 %all-to-all-start = ((bf16[32,2,2048]{2,1,0:T(2,128)(2,1)}), bf16[32,2,2048]{2,1,0:T(2,128)(2,1)S(1)}, u32[]{:S(2)}, u32[]{:S(2)}) async-start(bf16[32,2,2048]{2,1,0:T(2,128)(2,1)} %reshape.196), calls=%async_computation | async-start | bytes 524288 | tf_op jit(solution)/shard_map/all_to_all | solution.py:80
  23.6 12.3 %copy-start.4 = (s32[1,4096]{1,0:T(1,128)S(1)}, s32[1,4096]{1,0:T(1,128)}, u32[]{:S(2)}) copy-start(s32[1,4096]{1,0:T(1,128)} %param.12) | copy-start | bytes 49156
  23.6 12.7 %copy-start.5 = (s32[1,32]{1,0:T(1,128)S(1)}, s32[1,32]{1,0:T(1,128)}, u32[]{:S(2)}) copy-start(s32[1,32]{1,0:T(1,128)} %param.13) | copy-start | bytes 388
  32.1 33.2 %all-to-all-start.3 = ((bf16[128,32,256]{2,0,1:T(8,128)(2,1)}), bf16[128,32,256]{2,0,1:T(8,128)(2,1)S(1)}, u32[]{:S(2)}, u32[]{:S(2)}) async-start(bf16[128,32,256]{2,0,1:T(8,128)(2,1)} %copy.27), calls=%async_computation.3 | async-start | bytes 4194304 | tf_op jit(solution)/shard_map/all_to_all | solution.py:68
  65.2 39.9 %all-to-all-start.1 = ((bf16[32,256,64]{1,2,0:T(8,128)(2,1)}), bf16[32,256,64]{1,2,0:T(8,128)(2,1)}, u32[]{:S(2)}, u32[]{:S(2)}) async-start(bf16[32,256,64]{1,2,0:T(8,128)(2,1)} %copy.25), calls=%async_computation.1 | async-start | bytes 2097152 | tf_op jit(solution)/shard_map/all_to_all | solution.py:79
  341.0 39.9 %copy-start.1 = (bf16[32,256,64]{1,2,0:T(8,128)(2,1)S(1)}, bf16[32,256,64]{1,2,0:T(8,128)(2,1)}, u32[]{:S(2)}) copy-start(bf16[32,256,64]{1,2,0:T(8,128)(2,1)} %copy.23) | copy-start | bytes 3145732
  341.1 39.9 %copy-start.6 = (bf16[32,256,64]{1,2,0:T(8,128)(2,1)S(1)}, bf16[32,256,64]{1,2,0:T(8,128)(2,1)}, u32[]{:S(2)}) copy-start(bf16[32,256,64]{1,2,0:T(8,128)(2,1)} %get-tuple-element.8) | copy-start | bytes 3145732
  378.1 8.3 %copy-start.3 = (bf16[32,256,64]{1,2,0:T(8,128)(2,1)S(1)}, bf16[32,256,64]{1,2,0:T(8,128)(2,1)}, u32[]{:S(2)}) copy-start(bf16[32,256,64]{1,2,0:T(8,128)(2,1)} %get-tuple-element.7) | copy-start | bytes 3145732
  379.6 49.8 %collective-permute-start = (bf16[128,8192]{1,0:T(8,128)(2,1)}, bf16[128,8192]{1,0:T(8,128)(2,1)}, u32[]{:S(2)}, u32[]{:S(2)}) collective-permute-start(bf16[128,8192]{1,0:T(8,128)(2,1)} %bitcast.25), channel_id=1, source_target_pairs={{32,0},{64,32},{96,64},{128,96},{160,128},{192,160},{224,192},{33,... | collective-permute-start | bytes 6291464 | tf_op jit(solution)/shard_map/ppermute | solution.py:14
  382.5 12.9 %all-to-all-start.5 = ((bf16[32,2,2048]{2,1,0:T(2,128)(2,1)}), bf16[32,2,2048]{2,1,0:T(2,128)(2,1)S(1)}, u32[]{:S(2)}, u32[]{:S(2)}) async-start(bf16[32,2,2048]{2,1,0:T(2,128)(2,1)} %reshape.198), calls=%async_computation.5 | async-start | bytes 524288 | tf_op jit(solution)/shard_map/all_to_all | solution.py:123
  395.4 20.8 %all-to-all-start.4 = ((bf16[256,32,64]{0,2,1:T(8,128)(2,1)}), bf16[256,32,64]{0,2,1:T(8,128)(2,1)S(1)}, u32[]{:S(2)}, u32[]{:S(2)}) async-start(bf16[256,32,64]{0,2,1:T(8,128)(2,1)} %fusion.12), calls=%async_computation.4 | async-start | bytes 2097152 | tf_op jit(solution)/shard_map/all_to_all | solution.py:122
Sparse Core Ops, SparseCore 0:
  10.6 111.3 all-gather.2
where the time goes:
time: 440 us; the launch traced here: 439 us
  blocking collectives  183 us (42%)
  local copies, waits for them, and re-layouts  110 us (25%)
  waiting for transfers between devices  74.8 us (17%)
  matrix products  29.6 us (7%)
  starting transfers between devices  26.9 us (6%)
  between operations  14.3 us (3%)
    psum x1, blocking collectives, local(): up_total, down_total = lax.psum((up_part, down_part), 'dp')  146 us
    gather x3, local copies, waits for them, and re-layouts, masked_rows(): picked = rows[row_index]  65.3 us
    all_to_all x1, blocking collectives, local(): lax.all_to_all(input_columns, 'dp', split_axis=0, concat_axis=1, tiled=True)  37 us
    all_to_all x1, waiting for transfers between devices, local(): lax.all_to_all(saved_rows, 'dp', split_axis=1, concat_axis=0, tiled=True)  25.3 us
    gather x1, local copies, waits for them, and re-layouts, adapter_term(): blocks.reshape(blocks.shape[0] * blocks.shape[1], blocks.shape[2])  19.5 us
    all_to_all x1, waiting for transfers between devices, local(): lax.all_to_all(down_grad_cols, 'dp', split_axis=1, concat_axis=0, tiled=T...  15.1 us
    all_gather x1, waiting for transfers between devices, local(): block_rows = lax.all_gather(grad_rows, 'dp', axis=0, tiled=True)  12.3 us
    dot_general x1, matrix products, local(): lax.dot_general(block_rows, weight, contract_last, preferred_element_type...  11.8 us
  transfers between devices with their start and end apart: 7, of which 6 were waited for; matrix products, arithmetic and copies ran while one was open for 14% of the time, Pallas kernels for 0%

commit v1 on v0

--- a/solution.py
+++ b/solution.py
@@ -67,7 +67,9 @@
     )
     saved_cols = lax.all_to_all(saved_rows, "dp", split_axis=1, concat_axis=0, tiled=True)
     saved_input_blocks = masked_rows(saved_cols, row_index, live_slot)
-    block_rows = lax.all_gather(grad_rows, "dp", axis=0, tiled=True)
+    block_rows = jnp.concatenate(
+        lax.all_to_all(jnp.stack([grad_rows] * lax.axis_size("dp")), "dp", 0, 0), axis=0
+    )
     frozen_part = lax.dot_general(
         block_rows, weight, contract_last, preferred_element_type=jnp.float32
     )

time: 440 us -> 663 us (1.51)
  waiting for transfers between devices: 74.8 us -> 241 us
  blocking collectives: 183 us -> 246 us
  between operations: 14.3 us -> 0.88 us
  local copies, waits for them, and re-layouts: 110 us -> 117 us
    all_to_all x1, waiting for transfers between devices: 25.3 us -> 191 us  [local(): lax.all_to_all(jnp.stack([grad_rows] * lax.axis_size('dp')), 'dp', 0, 0)]
    all_to_all x0 -> x1, blocking collectives: none -> 32.1 us  [local(): lax.all_to_all(saved_rows, 'dp', split_axis=1, concat_axis=0, tiled=True)]
    psum x1, blocking collectives: 146 us -> 177 us  [local(): up_total, down_total = lax.psum((up_part, down_part), 'dp')]
    all_to_all x1, waiting for transfers between devices: 0.01 us -> 13.9 us  [local(): lax.all_to_all(adapter_down_maps[0], 'dp', split_axis=0, concat_axis=1, t...]
    all_gather x1 -> x0, waiting for transfers between devices: 12.3 us -> none  [local(): block_rows = lax.all_gather(grad_rows, 'dp', axis=0, tiled=True)]
    another operation x1 -> x2, local copies, waits for them, and re-layouts: 0.09 us -> 6.87 us  [the longest x1 6.78 us: local(): jnp.stack([grad_rows] * lax.axis_size('dp'))]
  transfers between devices with their start and end apart: 7 -> 6, of which waited for: 6 -> 6; matrix products, arithmetic and copies ran while one was open for 14% -> 8% of each run, Pallas kernels for 0% -> 0%
where the time goes in v1:
time: 663 us; the launch traced here: 662 us
  blocking collectives  246 us (37%)
  waiting for transfers between devices  241 us (36%)
  local copies, waits for them, and re-layouts  117 us (18%)
  matrix products  29.3 us (4%)
  starting transfers between devices  27.1 us (4%)
    all_to_all x1, waiting for transfers between devices, local(): lax.all_to_all(jnp.stack([grad_rows] * lax.axis_size('dp')), 'dp', 0, 0)  191 us
    psum x1, blocking collectives, local(): up_total, down_total = lax.psum((up_part, down_part), 'dp')  177 us
    gather x3, local copies, waits for them, and re-layouts, masked_rows(): picked = rows[row_index]  65.1 us
    all_to_all x1, blocking collectives, local(): lax.all_to_all(input_columns, 'dp', split_axis=0, concat_axis=1, tiled=True)  37 us
    all_to_all x1, blocking collectives, local(): lax.all_to_all(saved_rows, 'dp', split_axis=1, concat_axis=0, tiled=True)  32.1 us
    gather x1, local copies, waits for them, and re-layouts, adapter_term(): blocks.reshape(blocks.shape[0] * blocks.shape[1], blocks.shape[2])  19.5 us
    all_to_all x1, waiting for transfers between devices, local(): lax.all_to_all(down_grad_cols, 'dp', split_axis=1, concat_axis=0, tiled=T...  15.1 us
    all_to_all x1, waiting for transfers between devices, local(): lax.all_to_all(adapter_down_maps[0], 'dp', split_axis=0, concat_axis=1, t...  13.9 us
  transfers between devices with their start and end apart: 6, of which 6 were waited for; matrix products, arithmetic and copies ran while one was open for 8% of the time, Pallas kernels for 0%

profile of v1, /device:TPU:1, one launch (start us, length us, event | category | flops | bytes accessed | tf_op | source)
XLA Modules:
  0.0 661.8 jit_solution(4481902951639756754)
XLA Ops:
  0.6 2.4 all_to_all.76
  3.0 2.2 copy.35
  5.2 2.1 reshape.199
  7.3 8.6 %all-to-all-start.1 = ((bf16[32,2,2048]{2,1,0:T(2,128)(2,1)}), bf16[32,2,2048]{2,1,0:T(2,128)(2,1)S(1)}, u32[]{:S(2)}, u32[]{:S(2)}) async-start(bf16[32,2,2048]{2,1,0:T(2,128)(2,1)} %reshape.199), calls=%async_computation.1 | async-start | bytes 524288 | tf_op jit(solution)/shard_map/all_to_all | solution.py:82
  17.4 1.6 copy.25
  19.0 5.9 all-to-all-done.1
  24.9 4.5 all-to-all-start.2
  30.0 2.5 copy.27
  32.5 13.9 %all-to-all-done.2 = bf16[32,256,64]{1,2,0:T(8,128)(2,1)} async-done(((bf16[32,256,64]{1,2,0:T(8,128)(2,1)}), bf16[32,256,64]{1,2,0:T(8,128)(2,1)}, u32[]{:S(2)}, u32[]{:S(2)}) %all-to-all-start.2) | async-done | bytes 1048608 | tf_op jit(solution)/shard_map/all_to_all | solution.py:81
  46.4 32.1 %all_to_all.101 = bf16[128,32,256]{2,0,1:T(8,128)(2,1)S(1)} all-to-all(bf16[128,32,256]{2,0,1:T(8,128)(2,1)} %copy.27), channel_id=1, replica_groups=mesh['section'=8,'dp'=32] {'dp'}, dimensions={1} | all-to-all | bytes 4194304 | tf_op jit(solution)/shard_map/all_to_all | solution.py:68
  78.5 6.8 %stack.3 = bf16[32,128,2048]{2,1,0:T(8,128)(2,1)} broadcast(bf16[128,2048]{1,0:T(8,128)(2,1)} %bitcast.86), dimensions={1,2} | broadcast | bytes 17301504 | tf_op jit(solution)/shard_map/stack | solution.py:71
  85.3 5.1 all-to-all-start
  92.6 32.9 %gather_fusion.2 = bf16[8192,256]{1,0:T(8,128)(2,1)} fusion(bf16[4096,256]{1,0:T(8,128)(2,1)S(1)} %bitcast.73, s32[8192]{0:T(1024)S(1)} %broadcast_clamp_fusion), kind=kCustom, calls=%fused_computation.2 | custom fusion | bytes 8421376 | tf_op jit(solution)/shard_map/gather | solution.py:36
  125.5 4.3 fusion.1
  129.8 190.7 %all-to-all-done = bf16[32,128,2048]{2,1,0:T(8,128)(2,1)} async-done(((bf16[32,128,2048]{2,1,0:T(8,128)(2,1)}), bf16[32,128,2048]{2,1,0:T(8,128)(2,1)}, u32[]{:S(2)}, u32[]{:S(2)}) %all-to-all-start) | async-done | bytes 16777248 | tf_op jit(solution)/shard_map/all_to_all | solution.py:71
  320.5 1.6 constant_dynamic-slice_fusion
  322.1 29.5 %gather_fusion = bf16[8192,64]{1,0:T(8,128)(2,1)} fusion(bf16[4096,64]{1,0:T(8,128)(2,1)S(1)} %constant_dynamic-slice_fusion, s32[8192]{0:T(1024)S(1)} %broadcast_clamp_fusion), kind=kCustom, calls=%fused_computation | custom fusion | bytes 2129920 | tf_op jit(solution)/shard_map/gather | solution.py:36
  351.6 2.7 copy.23
  354.3 1.8 fusion.13
  356.1 177.0 %all-reduce.2 = (bf16[32,256,64]{1,2,0:T(8,128)(2,1)}, bf16[32,256,64]{1,2,0:T(8,128)(2,1)}) all-reduce(f32[32,256,64]{1,2,0:T(8,128)S(1)} %fusion.13, f32[32,256,64]{1,2,0:T(8,128)} %fusion.1), channel_id=1, replica_groups=mesh['section'=8,'dp'=32] {'dp'}, use_global_device_ids=true, to_apply=%region_4.5 | all-reduce | flops 1048576 | bytes 6291456 | tf_op jit(solution)/shard_map/psum | solution.py:93
  533.1 6.1 fusion.9
  539.1 19.5 %gather_fusion.1 = f32[4096,256]{1,0:T(8,128)} fusion(f32[8192,256]{1,0:T(8,128)} %bitcast.74, s32[4096]{0:T(1024)S(1)} %broadcast_clamp_fusion.1), kind=kCustom, calls=%fused_computation.1 | custom fusion | bytes 8404992 | tf_op jit(solution)/shard_map/gather | solution.py:44
  558.6 11.8 %fusion = bf16[4096,256]{1,0:T(8,128)(2,1)S(1)} fusion(bf16[4096,2048]{1,0:T(8,128)(2,1)} %bitcast.1, f32[4096,256]{1,0:T(8,128)} %gather_fusion.1, bf16[1,256,2048]{2,1,0:T(8,128)(2,1)S(1)} %copy-done), kind=kOutput, calls=%fused_computation.4 | convolution fusion | flops 4298113024 | bytes 24117248 | tf_op jit(solution)/shard_map/dot_general | solution.py:73
  570.5 37.0 %all_to_all.102 = bf16[32,128,256]{2,1,0:T(8,128)(2,1)S(1)} all-to-all(bf16[32,128,256]{2,1,0:T(8,128)(2,1)S(1)} %bitcast.83), channel_id=1, replica_groups=mesh['section'=8,'dp'=32] {'dp'}, dimensions={0} | all-to-all | bytes 4194304 | tf_op jit(solution)/shard_map/all_to_all | solution.py:128
  607.5 1.5 copy.30
  611.9 3.9 all-to-all-start.6
  615.9 4.8 fusion.5
  620.7 4.2 all-to-all-done.6
  624.8 3.8 all-to-all-start.5
  630.5 15.1 %all-to-all-done.5 = bf16[256,32,64]{0,2,1:T(8,128)(2,1)S(1)} async-done(((bf16[256,32,64]{0,2,1:T(8,128)(2,1)}), bf16[256,32,64]{0,2,1:T(8,128)(2,1)S(1)}, u32[]{:S(2)}, u32[]{:S(2)}) %all-to-all-start.5) | async-done | bytes 1048608 | tf_op jit(solution)/shard_map/all_to_all | solution.py:124
  647.5 11.2 %collective-permute-done = bf16[128,8192]{1,0:T(8,128)(2,1)} collective-permute-done((bf16[128,8192]{1,0:T(8,128)(2,1)}, bf16[128,8192]{1,0:T(8,128)(2,1)}, u32[]{:S(2)}, u32[]{:S(2)}) %collective-permute-start) | collective-permute-done | bytes 2097184 | tf_op jit(solution)/shard_map/ppermute | solution.py:14
  658.7 3.1 copy.41
  (40 shorter events, 10.9 us)
Async XLA Ops:
  0.6 558.0 %copy-start = (bf16[1,256,2048]{2,1,0:T(8,128)(2,1)S(1)}, bf16[1,256,2048]{2,1,0:T(8,128)(2,1)}, u32[]{:S(2)}) copy-start(bf16[1,256,2048]{2,1,0:T(8,128)(2,1)} %param.9) | copy-start | bytes 3145732
  3.0 26.4 %copy-start.2 = (bf16[1,128,8192]{2,1,0:T(8,128)(2,1)S(1)}, bf16[1,128,8192]{2,1,0:T(8,128)(2,1)}, u32[]{:S(2)}) copy-start(bf16[1,128,8192]{2,1,0:T(8,128)(2,1)} %param.8) | copy-start | bytes 6291460
  7.3 17.6 %all-to-all-start.1 = ((bf16[32,2,2048]{2,1,0:T(2,128)(2,1)}), bf16[32,2,2048]{2,1,0:T(2,128)(2,1)S(1)}, u32[]{:S(2)}, u32[]{:S(2)}) async-start(bf16[32,2,2048]{2,1,0:T(2,128)(2,1)} %reshape.199), calls=%async_computation.1 | async-start | bytes 524288 | tf_op jit(solution)/shard_map/all_to_all | solution.py:82
  24.9 21.5 %all-to-all-start.2 = ((bf16[32,256,64]{1,2,0:T(8,128)(2,1)}), bf16[32,256,64]{1,2,0:T(8,128)(2,1)}, u32[]{:S(2)}, u32[]{:S(2)}) async-start(bf16[32,256,64]{1,2,0:T(8,128)(2,1)} %copy.25), calls=%async_computation.2 | async-start | bytes 2097152 | tf_op jit(solution)/shard_map/all_to_all | solution.py:81
  85.3 5.1 copy-start.4
  85.3 5.6 copy-start.5
  85.3 235.2 %all-to-all-start = ((bf16[32,128,2048]{2,1,0:T(8,128)(2,1)}), bf16[32,128,2048]{2,1,0:T(8,128)(2,1)}, u32[]{:S(2)}, u32[]{:S(2)}) async-start(bf16[32,128,2048]{2,1,0:T(8,128)(2,1)} %stack.3), calls=%async_computation | async-start | bytes 33554432 | tf_op jit(solution)/shard_map/all_to_all | solution.py:71
  570.5 39.9 %copy-start.1 = (bf16[32,256,64]{1,2,0:T(8,128)(2,1)S(1)}, bf16[32,256,64]{1,2,0:T(8,128)(2,1)}, u32[]{:S(2)}) copy-start(bf16[32,256,64]{1,2,0:T(8,128)(2,1)} %copy.23) | copy-start | bytes 3145732
  570.5 39.9 %copy-start.6 = (bf16[32,256,64]{1,2,0:T(8,128)(2,1)S(1)}, bf16[32,256,64]{1,2,0:T(8,128)(2,1)}, u32[]{:S(2)}) copy-start(bf16[32,256,64]{1,2,0:T(8,128)(2,1)} %get-tuple-element.8) | copy-start | bytes 3145732
  607.5 8.3 %copy-start.3 = (bf16[32,256,64]{1,2,0:T(8,128)(2,1)S(1)}, bf16[32,256,64]{1,2,0:T(8,128)(2,1)}, u32[]{:S(2)}) copy-start(bf16[32,256,64]{1,2,0:T(8,128)(2,1)} %get-tuple-element.7) | copy-start | bytes 3145732
  609.0 49.7 %collective-permute-start = (bf16[128,8192]{1,0:T(8,128)(2,1)}, bf16[128,8192]{1,0:T(8,128)(2,1)}, u32[]{:S(2)}, u32[]{:S(2)}) collective-permute-start(bf16[128,8192]{1,0:T(8,128)(2,1)} %bitcast.25), channel_id=1, source_target_pairs={{32,0},{64,32},{96,64},{128,96},{160,128},{192,160},{224,192},{33,... | collective-permute-start | bytes 6291464 | tf_op jit(solution)/shard_map/ppermute | solution.py:14
  611.9 12.9 %all-to-all-start.6 = ((bf16[32,2,2048]{2,1,0:T(2,128)(2,1)}), bf16[32,2,2048]{2,1,0:T(2,128)(2,1)S(1)}, u32[]{:S(2)}, u32[]{:S(2)}) async-start(bf16[32,2,2048]{2,1,0:T(2,128)(2,1)} %reshape.201), calls=%async_computation.6 | async-start | bytes 524288 | tf_op jit(solution)/shard_map/all_to_all | solution.py:125
  624.8 20.8 %all-to-all-start.5 = ((bf16[256,32,64]{0,2,1:T(8,128)(2,1)}), bf16[256,32,64]{0,2,1:T(8,128)(2,1)S(1)}, u32[]{:S(2)}, u32[]{:S(2)}) async-start(bf16[256,32,64]{0,2,1:T(8,128)(2,1)} %fusion.5), calls=%async_computation.5 | async-start | bytes 2097152 | tf_op jit(solution)/shard_map/all_to_all | solution.py:124
